TPU v7x, 512 devices: a whole 4x4x16 slice. The times are simulated.
512 devices in a mesh: span: 64 (over z, x), seq: 8 (over y, core).
Axes of the slice: x: 4, y: 4, z: 16, core: 2. Of those that a mesh axis runs over, the one named last changes fastest.
Arguments:
- queries: bfloat16 [65536, 3072], P(('span', 'seq')), may hold values from -64 to 64
- keys: bfloat16 [65536, 3072], P(('span', 'seq')), may hold values from -4 to 4
- values: bfloat16 [65536, 3072], P(('span', 'seq')), may hold values from -6 to 6
- latent: bfloat16 [65536, 3072], P(('span', 'seq')), may hold values from -6 to 6
- fresh_noise: bfloat16 [1024, 3072], P('seq'), may hold values from -6 to 6
- pool_weight: bfloat16 [32, 24], replicated, may hold values from -1 to 1
- gate_table: bfloat16 [64, 3072], replicated, may hold values from -4 to 4
- levels: int32 [64], P('span'), may hold values from 0 to 63
Outputs:
- next_latent: bfloat16 [65536, 3072], P(('span', 'seq'))
All inputs are finite; a program needn't handle non-finite values.
Results may differ from a plain program's by a relative error of at most 0.005.
Values may be sent and summed in bfloat16 or wider, within the bound.
A program may use at most 64 MiB of HBM per device.

v0:
```python
import jax
import jax.numpy as jnp
from jax import lax
from jax.sharding import PartitionSpec as P

HEADS = 24
HEAD_DIM = 128
POOL = 32


neg_large = -1e30


def from_behind(shard, axis, by):
    size = lax.axis_size(axis)
    pairs = [(i, i + by) for i in range(size) if 0 <= i + by < size]
    return lax.ppermute(shard, axis, pairs)


def attend_block(state, query_block, key_rows, value_rows, valid):
    top_prev, total_prev, weighted_prev = state
    scores = jnp.einsum(
        "qhd,khd->qhk", query_block, key_rows, preferred_element_type=jnp.float32
    ) * HEAD_DIM ** (-0.5)
    scores = jnp.where(valid[None, None, :], scores, neg_large)
    top_next = jnp.maximum(top_prev, jnp.max(scores, axis=2))
    weights = jnp.where(valid[None, None, :], jnp.exp(scores - top_next[:, :, None]), 0.0)
    factor = jnp.exp(top_prev - top_next)
    total_next = factor * total_prev + jnp.sum(weights, axis=2)
    weighted_next = factor[:, :, None] * weighted_prev + jnp.einsum(
        "qhk,khd->qhd", weights.astype(jnp.bfloat16), value_rows, preferred_element_type=jnp.float32
    )
    return (top_next, total_next, weighted_next)


def attend_all(state, query_blocks, key_rows, value_rows, valid):

    def single(item):
        return attend_block(item[0], item[1], key_rows, value_rows, valid)

    return lax.map(single, (state, query_blocks))


def attend_where(state, query_blocks, key_rows, value_rows, valid):

    def active(current):
        return attend_all(current, query_blocks, key_rows, value_rows, valid)

    def passive(current):
        return current

    return lax.cond(jnp.any(valid), active, passive, state)


def local(queries, keys, values, latent, fresh_noise, pool_weight, gate_table, levels):
    seq_count = lax.axis_size("seq")
    span_index = lax.axis_index("span")
    seq_index = lax.axis_index("seq")
    heads_here = HEADS // seq_count
    width = heads_here * HEAD_DIM
    query_heads, key_heads, value_heads = (
        lax.all_to_all(queries, "seq", split_axis=1, concat_axis=0, tiled=True),
        lax.all_to_all(keys, "seq", split_axis=1, concat_axis=0, tiled=True),
        lax.all_to_all(values, "seq", split_axis=1, concat_axis=0, tiled=True),
    )
    span_len = query_heads.shape[0]
    block_len = min(512, span_len)
    block_count = span_len // block_len
    summary_len = span_len // POOL
    key_split = key_heads.reshape(span_len, heads_here, HEAD_DIM)
    value_split = value_heads.reshape(span_len, heads_here, HEAD_DIM)
    query_blocks = query_heads.reshape(block_count, block_len, heads_here, HEAD_DIM)
    mixing = lax.dynamic_slice_in_dim(pool_weight, seq_index * heads_here, heads_here, 1)
    key_summary = (
        jnp.einsum(
            "jphd,ph->jhd",
            key_split.reshape(summary_len, POOL, heads_here, HEAD_DIM),
            mixing,
            preferred_element_type=jnp.float32,
        )
        .astype(jnp.bfloat16)
        .reshape(summary_len, width)
    )
    value_summary = (
        jnp.einsum(
            "jphd,ph->jhd",
            value_split.reshape(summary_len, POOL, heads_here, HEAD_DIM),
            mixing,
            preferred_element_type=jnp.float32,
        )
        .astype(jnp.bfloat16)
        .reshape(summary_len, width)
    )
    all_valid = jnp.ones((span_len,), jnp.bool_)
    start_state = (
        jnp.full((block_count, block_len, heads_here), neg_large, jnp.float32),
        jnp.zeros((block_count, block_len, heads_here), jnp.float32),
        jnp.zeros((block_count, block_len, heads_here, HEAD_DIM), jnp.float32),
    )
    piece = (
        lax.all_gather(key_summary, "span", axis=0, tiled=True),
        lax.all_gather(value_summary, "span", axis=0, tiled=True),
    )
    piece_rows = piece[0].shape[0]
    owner = jnp.arange(piece_rows, dtype=jnp.int32) // summary_len
    key_rows = piece[0].reshape(piece_rows, heads_here, HEAD_DIM)
    value_rows = piece[1].reshape(piece_rows, heads_here, HEAD_DIM)
    owner, key_rows, value_rows = (owner, key_rows, value_rows)
    state = attend_where(start_state, query_blocks, key_rows, value_rows, owner > span_index)
    state = attend_all(state, query_blocks, key_split, value_split, all_valid)
    finished = (state[2] / state[1][..., None]).astype(jnp.bfloat16).reshape(span_len, width)
    attention = lax.all_to_all(finished, "seq", split_axis=0, concat_axis=1, tiled=True).astype(
        jnp.float32
    )
    inverse = lax.rsqrt(jnp.mean(attention * attention, axis=1, keepdims=True) + 1e-06)
    level_now = levels[0]
    selector = (jnp.arange(gate_table.shape[0], dtype=jnp.int32) == level_now).astype(jnp.bfloat16)
    gate_row = jnp.dot(selector[None, :], gate_table, preferred_element_type=jnp.float32)
    sigma = (level_now.astype(jnp.float32) + 1.0) / gate_table.shape[0]
    cleaned = (latent.astype(jnp.float32) - sigma * gate_row * attention * inverse).astype(
        jnp.bfloat16
    )
    moved = from_behind(cleaned, "span", 1)
    return jnp.where(span_index == 0, fresh_noise, moved)


def solution(mesh):
    placed = (
        P(("span", "seq"), None),
        P(("span", "seq"), None),
        P(("span", "seq"), None),
        P(("span", "seq"), None),
        P("seq", None),
        P(),
        P(),
        P("span"),
    )
    return jax.shard_map(
        local, mesh=mesh, in_specs=placed, out_specs=P(("span", "seq"), None), check_vma=False
    )
```

profile of v0, /device:TPU:32, one launch (start us, length us, event | category | flops | bytes accessed | tf_op | source)
XLA Modules:
  0.0 413.2 jit_solution(3030915349568692666)
XLA Ops:
  6.5 2.3 copy.44
  8.9 4.5 %all-to-all-start = ((bf16[128,8,384]{0,2,1:T(8,128)(2,1)}), bf16[128,8,384]{0,2,1:T(8,128)(2,1)S(1)}, u32[]{:S(2)}, u32[]{:S(2)}) async-start(bf16[128,8,384]{0,2,1:T(8,128)(2,1)} %bitcast.20), calls=%async_computation | async-start | bytes 1572864 | tf_op jit(solution)/shard_map/all_to_all | solution.py:63
  14.1 12.4 %all-to-all-done = bf16[128,8,384]{0,2,1:T(8,128)(2,1)S(1)} async-done(((bf16[128,8,384]{0,2,1:T(8,128)(2,1)}), bf16[128,8,384]{0,2,1:T(8,128)(2,1)S(1)}, u32[]{:S(2)}, u32[]{:S(2)}) %all-to-all-start) | async-done | bytes 786464 | tf_op jit(solution)/shard_map/all_to_all | solution.py:63
  28.1 1.5 copy.46
  29.6 15.6 %all_to_all.61 = bf16[128,8,384]{0,2,1:T(8,128)(2,1)S(1)} all-to-all(bf16[128,8,384]{0,2,1:T(8,128)(2,1)S(1)} %bitcast.206), channel_id=1, replica_groups=mesh['span'=64,'seq'=8] {'seq'}, dimensions={1} | all-to-all | bytes 1572864 | tf_op jit(solution)/shard_map/all_to_all | solution.py:64
  46.3 2.4 reshape_reshape.7
  49.7 2.3 copy.48
  51.9 3.5 all-to-all-start.2
  58.6 9.9 %all-to-all-done.2 = bf16[128,8,384]{0,2,1:T(8,128)(2,1)S(1)} async-done(((bf16[128,8,384]{0,2,1:T(8,128)(2,1)}), bf16[128,8,384]{0,2,1:T(8,128)(2,1)S(1)}, u32[]{:S(2)}, u32[]{:S(2)}) %all-to-all-start.2) | async-done | bytes 786464 | tf_op jit(solution)/shard_map/all_to_all | solution.py:62
  74.6 95.3 %all-gather.3.cloned.1.call-done = bf16[2048,384]{1,0:T(8,128)(2,1)} async-done(((bf16[32,384]{1,0:T(8,128)(2,1)}), bf16[2048,384]{1,0:T(8,128)(2,1)}) %all-gather.3.cloned.1.call-update) | async-done | bytes 1572880 | tf_op jit(solution)/shard_map/all_gather | solution.py:101
  169.8 139.4 %all-gather.5.cloned.1.call-done = bf16[2048,384]{1,0:T(8,128)(2,1)} async-done(((bf16[32,384]{1,0:T(8,128)(2,1)}), bf16[2048,384]{1,0:T(8,128)(2,1)}) %all-gather.5.cloned.1.call-update) | async-done | bytes 1572880 | tf_op jit(solution)/shard_map/all_gather | solution.py:102
  309.2 34.8 %conditional.1 = (f32[2,512,3]{1,2,0:T(4,128)}, f32[2,512,3]{1,2,0:T(4,128)}, f32[2,512,3,128]{3,1,2,0:T(8,128)}) conditional(s32[]{:T(128)} %convert_element_type.49, () %tuple.21, (bf16[2048,384]{1,0:T(8,128)(2,1)}, bf16[2048,384]{1,0:T(8,128)(2,1)}, pred[2048]{0:T(1024)(128)(4,1)S(1)}, bf16[2,512,3,128]{1,0,3,2:T(2,128)(2,1)}) %tuple.77), branch_computations={%region_1.2_spmd, %region_2.7_spmd} | conditional | flops 1651711488 | bytes 62613216 | solution.py:52
  309.2 2.6 copy.50
  311.9 1.9 copy.41
  313.8 2.6 copy.51
  316.4 2.6 copy.42
  319.0 3.1 copy.52
  322.1 22.0 %while.25 = (s32[]{:T(128)}, f32[2,512,3]{1,2,0:T(4,128)}, f32[2,512,3]{1,2,0:T(4,128)}, f32[2,512,3,128]{3,1,2,0:T(8,128)}, pred[2048]{0:T(1024)(128)(4,1)S(1)}...) while((s32[]{:T(128)}, f32[2,512,3]{1,2,0:T(4,128)}, ...), condition=%wide.region_6.6_spmd, body=%wide.region_3.5_spmd.sunk | while | flops 1651711488 | bytes 48457336 | solution.py:41
  322.1 3.2 bitcast_reduce_fusion.5
  325.2 3.9 fusion.108
  329.2 3.3 fusion.106
  333.0 3.2 bitcast_reduce_fusion.5
  336.2 3.9 fusion.108
  340.1 3.3 fusion.106
  344.0 14.5 %while.26 = (s32[]{:T(128)}, f32[2,512,3]{1,2,0:T(4,128)}, f32[2,512,3,128]{3,1,2,0:T(8,128)}, f32[2,512,3]{1,2,0:T(4,128)}, bf16[2,512,3,128]{3,1,2,0:T(8,128)(...) while((s32[]{:T(128)}, f32[2,512,3]{1,2,0:T(4,128)}, ...), condition=%wide.region_10.11_spmd, body=%wide.region_7.10_spmd.sunk | while | flops 818288640 | bytes 38336768 | solution.py:41
  345.8 2.7 fusion.102
  353.1 2.7 fusion.102
  358.5 1.9 divide_convert_fusion
  362.6 4.4 %all-to-all-start.3 = ((bf16[8,128,384]{1,2,0:T(8,128)(2,1)}), bf16[8,128,384]{1,2,0:T(8,128)(2,1)S(1)}, u32[]{:S(2)}, u32[]{:S(2)}) async-start(bf16[8,128,384]{1,2,0:T(8,128)(2,1)} %copy.59), calls=%async_computation.3 | async-start | bytes 1572864 | tf_op jit(solution)/shard_map/all_to_all | solution.py:112
  368.2 11.9 %all-to-all-done.3 = bf16[8,128,384]{1,2,0:T(8,128)(2,1)S(1)} async-done(((bf16[8,128,384]{1,2,0:T(8,128)(2,1)}), bf16[8,128,384]{1,2,0:T(8,128)(2,1)S(1)}, u32[]{:S(2)}, u32[]{:S(2)}) %all-to-all-start.3) | async-done | bytes 786464 | tf_op jit(solution)/shard_map/all_to_all | solution.py:112
  381.9 2.9 collective-permute-start
  385.3 19.8 %collective-permute-done = bf16[128,3072]{0,1:T(8,128)(2,1)S(1)} collective-permute-done((bf16[128,3072]{0,1:T(8,128)(2,1)}, bf16[128,3072]{0,1:T(8,128)(2,1)S(1)}, u32[]{:S(2)}, u32[]{:S(2)}) %collective-permute-start) | collective-permute-done | bytes 786464 | tf_op jit(solution)/shard_map/ppermute | solution.py:17
  (87 shorter events, 29.2 us)
Async XLA Ops:
  6.5 361.5 %copy-start = (bf16[64,3072]{1,0:T(8,128)(2,1)S(1)}, bf16[64,3072]{1,0:T(8,128)(2,1)}, u32[]{:S(2)}) copy-start(bf16[64,3072]{1,0:T(8,128)(2,1)} %param.20) | copy-start | bytes 1179652
  8.9 17.6 %all-to-all-start = ((bf16[128,8,384]{0,2,1:T(8,128)(2,1)}), bf16[128,8,384]{0,2,1:T(8,128)(2,1)S(1)}, u32[]{:S(2)}, u32[]{:S(2)}) async-start(bf16[128,8,384]{0,2,1:T(8,128)(2,1)} %bitcast.20), calls=%async_computation | async-start | bytes 1572864 | tf_op jit(solution)/shard_map/all_to_all | solution.py:63
  13.3 156.5 %all-gather.3.cloned.1.call-start = ((), (), s32[]{:S(2)}) async-start(), calls=%async_computation.4 | async-start | bytes 1597440 | tf_op jit(solution)/shard_map/all_gather | solution.py:101
  28.0 281.2 %all-gather.5.cloned.1.call-start = ((), (), s32[]{:S(2)}) async-start(), calls=%async_computation.5 | async-start | bytes 1597440 | tf_op jit(solution)/shard_map/all_gather | solution.py:102
  51.9 16.6 %all-to-all-start.2 = ((bf16[128,8,384]{0,2,1:T(8,128)(2,1)}), bf16[128,8,384]{0,2,1:T(8,128)(2,1)S(1)}, u32[]{:S(2)}, u32[]{:S(2)}) async-start(bf16[128,8,384]{0,2,1:T(8,128)(2,1)} %bitcast.28), calls=%async_computation.2 | async-start | bytes 1572864 | tf_op jit(solution)/shard_map/all_to_all | solution.py:62
  69.1 1.2 copy-start.2
  69.4 0.9 copy-start.1
  322.1 3.2 copy-start.5
  333.0 3.2 copy-start.5
  344.0 1.8 copy-start.3
  344.0 1.8 copy-start.8
  348.6 1.4 copy-start.4
  348.6 1.4 copy-start.9
  350.7 0.6 copy-start.10
  351.3 1.8 copy-start.3
  351.3 1.8 copy-start.8
  355.8 1.4 copy-start.4
  355.8 1.4 copy-start.9
  357.9 0.6 copy-start.10
  360.4 7.3 %copy-start.6 = (bf16[128,3072]{1,0:T(8,128)(2,1)S(1)}, bf16[128,3072]{1,0:T(8,128)(2,1)}, u32[]{:S(2)}) copy-start(bf16[128,3072]{1,0:T(8,128)(2,1)} %param.17) | copy-start | bytes 2359300
  362.6 22.3 %copy-start.7 = (bf16[128,3072]{1,0:T(8,128)(2,1)S(1)}, bf16[128,3072]{1,0:T(8,128)(2,1)}, u32[]{:S(2)}) copy-start(bf16[128,3072]{1,0:T(8,128)(2,1)} %param.18) | copy-start | bytes 2359300
  362.6 17.6 %all-to-all-start.3 = ((bf16[8,128,384]{1,2,0:T(8,128)(2,1)}), bf16[8,128,384]{1,2,0:T(8,128)(2,1)S(1)}, u32[]{:S(2)}, u32[]{:S(2)}) async-start(bf16[8,128,384]{1,2,0:T(8,128)(2,1)} %copy.59), calls=%async_computation.3 | async-start | bytes 1572864 | tf_op jit(solution)/shard_map/all_to_all | solution.py:112
  381.9 23.2 %collective-permute-start = (bf16[128,3072]{0,1:T(8,128)(2,1)}, bf16[128,3072]{0,1:T(8,128)(2,1)S(1)}, u32[]{:S(2)}, u32[]{:S(2)}) collective-permute-start(bf16[128,3072]{0,1:T(8,128)(2,1)} %fusion.61), channel_id=1, source_target_pairs={{0,8},{8,16},{16,24},{24,32},{32,40},{40,48},{48,56},{56,64},{64,7... | collective-permute-start | bytes 2359304 | tf_op jit(solution)/shard_map/ppermute | solution.py:17
Sparse Core Ops, SparseCore 0:
  28.1 141.6 all-gather.2
  172.8 136.4 all-gather.4
where the time goes:
time: 414 us; the launch traced here: 413 us
  waiting for transfers between devices  289 us (70%)
  local copies, waits for them, and re-layouts  38.3 us (9%)
  matrix products  22.3 us (5%)
  other arithmetic  17.7 us (4%)
  blocking collectives  15.6 us (4%)
  starting transfers between devices  15.5 us (4%)
  between operations  14.9 us (4%)
    all_gather x1, waiting for transfers between devices, local(): lax.all_gather(value_summary, 'span', axis=0, tiled=True)  139 us
    all_gather x1, waiting for transfers between devices, local(): lax.all_gather(key_summary, 'span', axis=0, tiled=True)  95.3 us
    ppermute x1, waiting for transfers between devices, from_behind(): return lax.ppermute(shard, axis, pairs)  19.8 us
    all_to_all x1, blocking collectives, local(): lax.all_to_all(values, 'seq', split_axis=1, concat_axis=0, tiled=True)  15.6 us
    dot_general x4, matrix products, attend_block(): jnp.einsum('qhk,khd->qhd', weights.astype(jnp.bfloat16), value_rows, pref...  13.2 us
    all_to_all x1, waiting for transfers between devices, local(): lax.all_to_all(keys, 'seq', split_axis=1, concat_axis=0, tiled=True)  12.4 us
    all_to_all x1, waiting for transfers between devices, local(): lax.all_to_all(finished, 'seq', split_axis=0, concat_axis=1, tiled=True)  11.9 us
    all_to_all x1, waiting for transfers between devices, local(): lax.all_to_all(queries, 'seq', split_axis=1, concat_axis=0, tiled=True)  9.94 us
  transfers between devices with their start and end apart: 6, of which 6 were waited for; matrix products, arithmetic and copies ran while one was open for 4% of the time, Pallas kernels for 0%

commit v1 on v0

v1 whole, which is shorter than its diff:
```python
import functools
import math

import jax
import jax.numpy as jnp
from jax import lax
from jax.experimental import pallas as pl
from jax.experimental.pallas import tpu as pltpu
from jax.sharding import PartitionSpec as P

HEAD_DIM = 128
POOL = 32
CHUNKS = 4
NX = 4
MESH = pl.DeviceIdType.MESH
F32 = jnp.float32
BF16 = jnp.bfloat16


def kernel(
    nz, nx, ns, heads,
    q_ref, k_ref, v_ref, lat_ref, fresh_ref, pool_ref, gate_ref, lev_ref, out_ref,
    qbuf, kbuf, vbuf, sum_send, sum_recv, sbuf, m_buf, acc_buf, obuf, att, lat, cbuf, shift, coef,
    qkv_s, qkv_r, loc, ss, sr, xs, xr, ds_, dr, us, ur, os_, or_, hs_, hr, fin,
):
    nsp = nz * nx
    hl = heads // ns
    width = hl * HEAD_DIM
    tl = k_ref.shape[0]
    rows = tl // CHUNKS
    groups = tl // POOL
    gr = groups * ns
    cs = nz // 4
    nd, nu = nz // 2, nz // 2 - 1
    qn = ns * rows
    c_exp = HEAD_DIM ** (-0.5) * math.log2(math.e)

    span = lax.axis_index("span")
    seq = lax.axis_index("seq")
    z = lax.div(span, nx)
    x = lax.rem(span, nx)
    zdn = lax.rem(z + nz - 1, nz) * nx + x
    zup = lax.rem(z + 1, nz) * nx + x
    nxt = lax.rem(span + 1, nsp)
    prv = lax.rem(span + nsp - 1, nsp)

    def peer(o):
        return lax.rem(seq + o, ns)

    def source(o):
        return lax.rem(seq + ns - o, ns)

    def head_cols(s):
        return pl.ds(pl.multiple_of(s * width, HEAD_DIM), width)

    def remote(src, dst, send, recv, s, q):
        return pltpu.make_async_remote_copy(
            src_ref=src, dst_ref=dst, send_sem=send, recv_sem=recv, device_id=(s, q), device_id_type=MESH
        )

    def clear(i, carry):
        for part in range(2):
            sbuf[part, i] = jnp.zeros(sbuf.shape[2:], BF16)
        return carry

    lax.fori_loop(0, nz, clear, 0)

    barrier = pltpu.get_barrier_semaphore()

    def greet(s, q):
        pl.semaphore_signal(barrier, inc=1, device_id=(s, q), device_id_type=MESH)

    for o in range(1, ns):
        greet(span, peer(o))
    for o in range(1, nx):
        greet(z * nx + lax.rem(x + o, nx), seq)
    for s in (zdn, zup, nxt, prv):
        greet(s, seq)

    lat_copy = pltpu.make_async_copy(lat_ref, lat, loc.at[4])
    lat_copy.start()
    fresh_copy = pltpu.make_async_copy(fresh_ref, shift, loc.at[5])

    @pl.when(span == 0)
    def _():
        fresh_copy.start()

    pl.semaphore_wait(barrier, ns - 1 + nx - 1 + 4)

    def qkv_copy(t, o):
        d = peer(o)
        if t == 1:
            src, dst = q_ref.at[:, :, head_cols(d)], qbuf.at[:, seq]
        else:
            src, dst = (k_ref, v_ref)[t // 2].at[:, head_cols(d)], (kbuf, vbuf)[t // 2].at[seq]
        return remote(src, dst, qkv_s.at[t, o], qkv_r.at[t, o], span, d)

    def qkv_arrival(t, o):
        s = source(o)
        if t == 1:
            dst = qbuf.at[:, s]
        else:
            dst = (kbuf, vbuf)[t // 2].at[s]
        return pltpu.make_async_copy(dst, dst, qkv_r.at[t, o])

    own = (
        pltpu.make_async_copy(k_ref.at[:, head_cols(seq)], kbuf.at[seq], loc.at[0]),
        pltpu.make_async_copy(q_ref.at[:, :, head_cols(seq)], qbuf.at[:, seq], loc.at[1]),
        pltpu.make_async_copy(v_ref.at[:, head_cols(seq)], vbuf.at[seq], loc.at[2]),
    )

    for h in range(heads):
        cols = slice(h * HEAD_DIM, (h + 1) * HEAD_DIM)
        w = jnp.broadcast_to(pool_ref[:, h : h + 1].astype(F32), (POOL, HEAD_DIM))
        parts = []
        for ref in (k_ref, v_ref):
            grouped = ref[:, cols].astype(F32).reshape(groups, POOL, HEAD_DIM)
            parts.append(jnp.sum(grouped * w[None], axis=1))
        block = jnp.concatenate(parts, axis=0).astype(BF16)
        sum_send[h // hl, :, (h % hl) * HEAD_DIM : (h % hl + 1) * HEAD_DIM] = block

    def sum_copy(o):
        return remote(sum_send.at[peer(o)], sum_recv.at[seq], ss.at[o], sr.at[o], span, peer(o))

    def sum_arrival(o):
        dst = sum_recv.at[source(o)]
        return pltpu.make_async_copy(dst, dst, sr.at[o])

    own_sum = pltpu.make_async_copy(sum_send.at[seq], sum_recv.at[seq], loc.at[3])
    own_sum.start()
    for o in range(1, ns):
        sum_copy(o).start()
    for t in range(3):
        own[t].start()
        for o in range(1, ns):
            qkv_copy(t, o).start()

    level = lev_ref[0]
    sigma = (level.astype(F32) + 1.0) / gate_ref.shape[0]
    row_id = lax.broadcasted_iota(jnp.int32, gate_ref.shape, 0)
    row = jnp.sum(jnp.where(row_id == level, gate_ref[...].astype(F32), 0.0), axis=0, keepdims=True)
    coef[...] = jnp.broadcast_to(row * sigma, coef.shape)

    own_sum.wait()
    for o in range(1, ns):
        sum_arrival(o).wait()
    stacked = sum_recv[...].reshape(ns * 2 * groups, width)
    to_row = lax.broadcasted_iota(jnp.int32, (2 * gr, 2 * gr), 0)
    from_row = lax.broadcasted_iota(jnp.int32, (2 * gr, 2 * gr), 1)
    is_value = (to_row >= gr).astype(jnp.int32)
    within = to_row - is_value * gr
    wanted = (within // groups) * (2 * groups) + is_value * groups + within % groups
    order = (from_row == wanted).astype(F32).astype(BF16)
    sorted_rows = jnp.dot(order, stacked, preferred_element_type=F32).astype(BF16)
    sbuf[0, 0, x] = sorted_rows[:gr]
    sbuf[1, 0, x] = sorted_rows[gr:]

    def x_copy(o):
        return remote(
            sbuf.at[:, 0, x], sbuf.at[:, 0, x], xs.at[o], xr.at[o], z * nx + lax.rem(x + o, nx), seq
        )

    def x_arrival(o):
        dst = sbuf.at[:, 0, lax.rem(x + nx - o, nx)]
        return pltpu.make_async_copy(dst, dst, xr.at[o])

    for o in range(1, nx):
        x_copy(o).start()

    def down_copy(k, part):
        return remote(
            sbuf.at[part, k - 1], sbuf.at[part, k], ds_.at[k, part], dr.at[k, part], zdn, seq
        )

    def up_copy(k, part):
        return remote(
            sbuf.at[part, (nz + 1 - k) % nz], sbuf.at[part, nz - k], us.at[k, part], ur.at[k, part], zup, seq
        )

    def down_sends(k):
        return jnp.logical_and(z >= 1, z + k <= nz)

    def up_sends(k):
        return lax.rem(z - k + 1 + nz, nz) >= nz - nu

    def arrival(sem, slot, part):
        dst = sbuf.at[part, slot]
        return pltpu.make_async_copy(dst, dst, sem)

    for o in range(1, nx):
        x_arrival(o).wait()
    for part in range(2):

        @pl.when(down_sends(1))
        def _():
            down_copy(1, part).start()

        @pl.when(up_sends(1))
        def _():
            up_copy(1, part).start()

    def relay(k):
        for part in range(2):

            @pl.when(z + k <= nz - 1)
            def _():
                arrival(dr.at[k, part], k, part).wait()
                if k < nd:

                    @pl.when(z >= 1)
                    def _():
                        down_copy(k + 1, part).start()

            if k <= nu:

                @pl.when(lax.rem(z - k + nz, nz) >= nz - nu)
                def _():
                    arrival(ur.at[k, part], nz - k, part).wait()
                    if k < nu:
                        up_copy(k + 1, part).start()

    def head_slice(h):
        return slice(h * HEAD_DIM, (h + 1) * HEAD_DIM)

    def with_ones(v):
        return jnp.concatenate([v, jnp.ones(v.shape, v.dtype)], axis=1)

    def score(h, j, k):
        q = qbuf[j, :, :, head_slice(h)].reshape(qn, HEAD_DIM)
        return lax.dot_general(q, k, (((1,), (1,)), ((), ())), preferred_element_type=F32)

    def own_step(h, j):
        s = score(h, j, kbuf[:, :, head_slice(h)].reshape(ns * tl, HEAD_DIM))
        top = jnp.max(s, axis=1, keepdims=True)
        p = jnp.exp2((s - top) * c_exp).astype(BF16)
        v = with_ones(vbuf[:, :, head_slice(h)].reshape(ns * tl, HEAD_DIM))
        acc_buf[h, j] = jnp.dot(p, v, preferred_element_type=F32)
        m_buf[h, j] = jnp.broadcast_to(top, (qn, HEAD_DIM))

    def past_step(h, j, chunk):
        count = cs * nx * gr
        slots = pl.ds(chunk * cs, cs)
        s = score(h, j, sbuf[0, slots, :, :, head_slice(h)].reshape(count, HEAD_DIM))
        at = lax.broadcasted_iota(jnp.int32, (1, count), 1)
        ahead = chunk * cs * nx + at // gr
        valid = jnp.logical_and(ahead > x, z * nx + ahead < nsp)
        s = s + jnp.where(valid, 0.0, -1e30)
        before = m_buf[h, j][:, :1]
        top = jnp.maximum(before, jnp.max(s, axis=1, keepdims=True))
        p = jnp.exp2((s - top) * c_exp).astype(BF16)
        factor = jnp.exp2((before - top) * c_exp)
        v = with_ones(sbuf[1, slots, :, :, head_slice(h)].reshape(count, HEAD_DIM))
        acc_buf[h, j] = acc_buf[h, j] * factor + jnp.dot(p, v, preferred_element_type=F32)
        m_buf[h, j] = jnp.broadcast_to(top, (qn, HEAD_DIM))

    def first_pass(h):
        def step(j, carry):
            own_step(h, j)
            past_step(h, j, 0)

            @pl.when(z + 3 * cs <= nz - 1)
            def _():
                past_step(h, j, 3)

            return carry

        lax.fori_loop(0, CHUNKS, step, 0)

    last_relay = nd
    early = max(1, min(nd, cs + 1))
    for k in range(1, early + 1):
        relay(k)
    for t in range(3):
        own[t].wait()
        for o in range(1, ns):
            qkv_arrival(t, o).wait()
    for h in range(hl):
        first_pass(h)
        if early + 1 + h <= nd:
            relay(early + 1 + h)
    for k in range(early + 1 + hl, last_relay + 1):
        relay(k)

    def out_copy(j, o):
        return remote(obuf.at[j, peer(o)], att.at[j, seq], os_.at[j, o], or_.at[j, o], span, peer(o))

    def out_arrival(j, o):
        dst = att.at[j, source(o)]
        return pltpu.make_async_copy(dst, dst, or_.at[j, o])

    def own_out(j):
        return pltpu.make_async_copy(obuf.at[j, seq], att.at[j, seq], os_.at[j, 0])

    def shift_copy(j):
        return remote(cbuf.at[j], shift.at[j], hs_.at[j], hr.at[j], nxt, seq)

    def shift_arrival(j):
        return pltpu.make_async_copy(shift.at[j], shift.at[j], hr.at[j])

    lat_copy.wait()

    def second_pass(j):
        for h in range(hl):
            for chunk in (1, 2):

                @pl.when(z + chunk * cs <= nz - 1)
                def _():
                    past_step(h, j, chunk)

            acc = acc_buf[h, j]
            o = (acc[:, :HEAD_DIM] / acc[:, HEAD_DIM:]).astype(BF16)
            obuf[j, :, :, head_slice(h)] = o.reshape(ns, rows, HEAD_DIM)
        own_out(j).start()
        for o in range(1, ns):
            out_copy(j, o).start()

    def finish(j):
        own_out(j).wait()
        for o in range(1, ns):
            out_arrival(j, o).wait()
        square = jnp.zeros((rows, HEAD_DIM), F32)
        for s in range(ns):
            for h in range(hl):
                a = att[j, s, :, head_slice(h)].astype(F32)
                square = square + a * a
        mean = jnp.sum(square, axis=1, keepdims=True) / (heads * HEAD_DIM)
        inverse = jnp.broadcast_to(lax.rsqrt(mean + 1e-06), (rows, HEAD_DIM))
        for s in range(ns):
            for h in range(hl):
                cols = slice((s * hl + h) * HEAD_DIM, (s * hl + h + 1) * HEAD_DIM)
                a = att[j, s, :, head_slice(h)].astype(F32)
                cleaned = lat[j, :, cols].astype(F32) - coef[:1, cols] * a * inverse
                cbuf[j, :, cols] = cleaned.astype(BF16)

        @pl.when(span < nsp - 1)
        def _():
            shift_copy(j).start()

    def tail(j, carry):
        @pl.when(j < CHUNKS)
        def _():
            second_pass(j)

        @pl.when(j >= 1)
        def _():
            finish(j - 1)

        return carry

    lax.fori_loop(0, CHUNKS + 1, tail, 0)

    @pl.when(span == 0)
    def _():
        fresh_copy.wait()

    def leave(j):
        return pltpu.make_async_copy(shift.at[j], out_ref.at[j], fin.at[j])

    for j in range(CHUNKS):

        @pl.when(span > 0)
        def _():
            shift_arrival(j).wait()

        leave(j).start()

    for t in range(3):
        for o in range(1, ns):
            qkv_copy(t, o).wait_send()
    for o in range(1, ns):
        sum_copy(o).wait_send()
    for o in range(1, nx):
        x_copy(o).wait_send()
    for part in range(2):
        for k in range(1, nd + 1):

            @pl.when(down_sends(k))
            def _():
                down_copy(k, part).wait_send()

        for k in range(1, nu + 1):

            @pl.when(up_sends(k))
            def _():
                up_copy(k, part).wait_send()

    for j in range(CHUNKS):
        for o in range(1, ns):
            out_copy(j, o).wait_send()

        @pl.when(span < nsp - 1)
        def _():
            shift_copy(j).wait_send()

        leave(j).wait()


def local(nz, nx, queries, keys, values, latent, fresh_noise, pool_weight, gate_table, levels):
    ns = lax.axis_size("seq")
    tl, channels = keys.shape
    heads = channels // HEAD_DIM
    hl = heads // ns
    width = hl * HEAD_DIM
    rows = tl // CHUNKS
    groups = tl // POOL
    gr = groups * ns
    qn = ns * rows
    nd = nz // 2
    split = (CHUNKS, rows, channels)
    vmem = pl.BlockSpec(memory_space=pltpu.VMEM)
    far = pl.BlockSpec(memory_space=pl.ANY)
    dma = pltpu.SemaphoreType.DMA
    out = pl.pallas_call(
        functools.partial(kernel, nz, nx, ns, heads),
        out_shape=jax.ShapeDtypeStruct(split, BF16),
        in_specs=[far, vmem, vmem, far, far, vmem, vmem, pl.BlockSpec(memory_space=pltpu.SMEM)],
        out_specs=far,
        scratch_shapes=[
            pltpu.VMEM((CHUNKS, ns, rows, width), BF16),
            pltpu.VMEM((ns, tl, width), BF16),
            pltpu.VMEM((ns, tl, width), BF16),
            pltpu.VMEM((ns, 2 * groups, width), BF16),
            pltpu.VMEM((ns, 2 * groups, width), BF16),
            pltpu.VMEM((2, nz, nx, gr, width), BF16),
            pltpu.VMEM((hl, CHUNKS, qn, HEAD_DIM), F32),
            pltpu.VMEM((hl, CHUNKS, qn, 2 * HEAD_DIM), F32),
            pltpu.VMEM((CHUNKS, ns, rows, width), BF16),
            pltpu.VMEM((CHUNKS, ns, rows, width), BF16),
            pltpu.VMEM(split, BF16),
            pltpu.VMEM(split, BF16),
            pltpu.VMEM(split, BF16),
            pltpu.VMEM((8, channels), F32),
            dma((3, ns)),
            dma((3, ns)),
            dma((6,)),
            dma((ns,)),
            dma((ns,)),
            dma((nx,)),
            dma((nx,)),
            dma((nd + 1, 2)),
            dma((nd + 1, 2)),
            dma((nd + 1, 2)),
            dma((nd + 1, 2)),
            dma((CHUNKS, ns)),
            dma((CHUNKS, ns)),
            dma((CHUNKS,)),
            dma((CHUNKS,)),
            dma((CHUNKS,)),
        ],
        compiler_params=pltpu.CompilerParams(
            collective_id=0, has_side_effects=True, vmem_limit_bytes=60 * 1024 * 1024
        ),
        name="step",
    )(
        queries.reshape(split),
        keys,
        values,
        latent.reshape(split),
        fresh_noise.reshape(split),
        pool_weight,
        gate_table,
        levels,
    )
    return out.reshape(tl, channels)


def solution(mesh, nx=NX):
    placed = (
        P(("span", "seq"), None),
        P(("span", "seq"), None),
        P(("span", "seq"), None),
        P(("span", "seq"), None),
        P("seq", None),
        P(),
        P(),
        P("span"),
    )
    return jax.shard_map(
        functools.partial(local, mesh.shape["span"] // nx, nx),
        mesh=mesh,
        in_specs=placed,
        out_specs=P(("span", "seq"), None),
        check_vma=False,
    )
```

time: 414 us -> 105 us (0.25)
  waiting for transfers between devices: 289 us -> 0 us
  Pallas kernels: 0 us -> 101 us
  local copies, waits for them, and re-layouts: 38.3 us -> 2.77 us
  matrix products: 22.3 us -> 0 us
  other arithmetic: 17.7 us -> 0 us
  blocking collectives: 15.6 us -> 0 us
  starting transfers between devices: 15.5 us -> 0 us
  between operations: 14.9 us -> 0.68 us
    all_gather x2 -> x0, waiting for transfers between devices: 235 us -> none  [the longest x1 139 us: local(): lax.all_gather(value_summary, 'span', axis=0, tiled=True)]
    pallas_call x0 -> x1, Pallas kernels: none -> 101 us  [local(): pl.pallas_call(functools.partial(kernel, nz, nx, ns, heads), out_shape=ja...]
    all_to_all x3 -> x0, waiting for transfers between devices: 34.2 us -> none  [the longest x1 12.4 us: local(): lax.all_to_all(keys, 'seq', split_axis=1, concat_axis=0, tiled=True)]
    dot_general x11 -> x0, matrix products: 22.3 us -> none  [the longest x4 13.2 us: attend_block(): jnp.einsum('qhk,khd->qhd', weights.astype(jnp.bfloat16), value_rows, pref...]
    ppermute x1 -> x0, waiting for transfers between devices: 19.8 us -> none  [from_behind(): return lax.ppermute(shard, axis, pairs)]
    all_to_all x1 -> x0, blocking collectives: 15.6 us -> none  [local(): lax.all_to_all(values, 'seq', split_axis=1, concat_axis=0, tiled=True)]
    all_to_all x3 -> x0, starting transfers between devices: 12.4 us -> none  [the longest x1 4.47 us: local(): lax.all_to_all(keys, 'seq', split_axis=1, concat_axis=0, tiled=True)]
    another operation x5 -> x0, local copies, waits for them, and re-layouts: 11 us -> none
  transfers between devices with their start and end apart: 6 -> 0, of which waited for: 6 -> 0; matrix products, arithmetic and copies ran while one was open for 4% -> 0% of each run, Pallas kernels for 0% -> 0%
where the time goes in v1:
time: 105 us; the launch traced here: 104 us
  Pallas kernels  101 us (96%)
  local copies, waits for them, and re-layouts  2.77 us (3%)
    pallas_call x1, Pallas kernels, local(): pl.pallas_call(functools.partial(kernel, nz, nx, ns, heads), out_shape=ja...  101 us
    unnamed x4, local copies, waits for them, and re-layouts  2.77 us

profile of v1, /device:TPU:32, one launch (start us, length us, event | category | flops | bytes accessed | tf_op | source)
XLA Modules:
  0.0 104.5 jit_solution(5946872128582740166)
XLA Ops:
  0.0 0.0 copy-start
  0.7 0.0 copy-done
  0.7 0.7 copy.9.pool_ref
  1.4 101.0 %step.1 = bf16[4,32,3072]{2,1,0:T(8,128)(2,1)} custom-call(bf16[4,32,3072]{2,1,0:T(8,128)(2,1)} %bitcast.5, bf16[128,3072]{1,0:T(8,128)(2,1)} %k_ref.1, bf16[128,3072]{1,0:T(8,128)(2,1)} %v_ref.1, bf16[4,32,3072]{2,1,0:T(8,128)(2,1)} %bitcast.6, bf16[4,32,3072]{2,1,0:T(8,128)(2,1)} %bitcast.7, bf16[32,24]{1,0:T(8,128)(2,1)} %copy.9.pool_ref, ...), custom_call_target="tpu_custom_call" | custom-call | tf_op jit(solution)/shard_map/step/pallas_call | solution.py:413
  102.4 2.1 %copy.12 = bf16[128,3072]{1,0:T(8,128)(2,1)} copy(bf16[128,3072]{1,0:T(8,128)(2,1)} %bitcast.4) | data formatting | bytes 1572864
Async XLA Ops:
  0.0 0.7 copy-start

commit v2 on v1

v2 whole, which is shorter than its diff:
```python
import functools
import math

import jax
import jax.numpy as jnp
from jax import lax
from jax.experimental import pallas as pl
from jax.experimental.pallas import tpu as pltpu
from jax.sharding import PartitionSpec as P

HEAD_DIM = 128
POOL = 32
CHUNKS = 4
NX = 4
VMEM_LIMIT = 60 * 1024 * 1024
MESH = pl.DeviceIdType.MESH
F32 = jnp.float32
BF16 = jnp.bfloat16


def kernel(
    nz, nx, ns, heads,
    q_ref, k_ref, v_ref, lat_ref, pool_ref, gate_ref, lev_ref, out_ref,
    kin, vin, gin, qbuf, kbuf, vbuf, sum_send, sum_recv, sk, sv, m_buf, l_buf, acc_buf, obuf, att, lat, cbuf, coef,
    qkv_s, qkv_r, loc, ss, sr, kxs, kxr, kds, kdr, kus, kur, vds, vdr, vus, vur, vxs, vxr, os_, or_, hs_, hr,
):
    nsp = nz * nx
    hl = heads // ns
    tl = kin.shape[0]
    rows = tl // CHUNKS
    groups = tl // POOL
    gr = groups * ns
    plane = nx * gr
    width = hl * HEAD_DIM
    cs = nz // 4
    nd, nu = nz // 2, nz // 2 - 1
    qn = ns * rows
    c_exp = HEAD_DIM ** (-0.5) * math.log2(math.e)

    span = lax.axis_index("span")
    seq = lax.axis_index("seq")
    z = lax.div(span, nx)
    x = lax.rem(span, nx)
    zdn = lax.rem(z + nz - 1, nz) * nx + x
    zup = lax.rem(z + 1, nz) * nx + x
    nxt = lax.rem(span + 1, nsp)
    prv = lax.rem(span + nsp - 1, nsp)
    far_first = sorted(range(1, ns), key=lambda o: abs(o - ns // 2))
    sides = sorted(range(1, nx), key=lambda d: min(d, nx - d))

    def peer(o):
        return lax.rem(seq + o, ns)

    def source(o):
        return lax.rem(seq + ns - o, ns)

    def x_span(dx):
        return z * nx + lax.rem(x + dx, nx)

    def x_source(dx):
        return lax.rem(x + nx - dx, nx)

    def head_cols(s, h):
        return pl.ds(pl.multiple_of((s * hl + h) * HEAD_DIM, HEAD_DIM), HEAD_DIM)

    def remote(src, dst, send, recv, s, q):
        return pltpu.make_async_remote_copy(
            src_ref=src, dst_ref=dst, send_sem=send, recv_sem=recv, device_id=(s, q), device_id_type=MESH
        )

    def landed(dst, sem):
        return pltpu.make_async_copy(dst, dst, sem)

    def load(i, src, dst):
        return pltpu.make_async_copy(src, dst, loc.at[i])

    loads = [load(0, k_ref, kin), load(1, v_ref, vin), load(2, gate_ref, gin), load(3, lat_ref, lat)]
    for c in loads:
        c.start()

    barrier = pltpu.get_barrier_semaphore()

    def greet(s, q):
        pl.semaphore_signal(barrier, inc=1, device_id=(s, q), device_id_type=MESH)

    for o in far_first:
        greet(span, peer(o))
    for s in (prv, zdn, zup):
        greet(s, seq)
    for dx in reversed(sides):
        greet(x_span(dx), seq)

    eye = lax.broadcasted_iota(jnp.int32, (POOL, POOL), 0) == lax.broadcasted_iota(jnp.int32, (POOL, POOL), 1)
    mixing = lax.dot_general(
        eye.astype(F32).astype(BF16), pool_ref[...], (((1,), (1,)), ((), ())), preferred_element_type=F32
    )
    loads[0].wait()
    loads[1].wait()
    for h in range(heads):
        cols = slice(h * HEAD_DIM, (h + 1) * HEAD_DIM)
        w = jnp.broadcast_to(mixing[:, h : h + 1], (POOL, HEAD_DIM))
        parts = []
        for ref in (kin, vin):
            grouped = ref[:, cols].astype(F32).reshape(groups, POOL, HEAD_DIM)
            parts.append(jnp.sum(grouped * w[None], axis=1))
        block = jnp.concatenate(parts, axis=0).astype(BF16)
        sum_send[h // hl, :, (h % hl) * HEAD_DIM : (h % hl + 1) * HEAD_DIM] = block

    pl.semaphore_wait(barrier, ns - 1 + 3 + nx - 1)

    def sum_copy(o):
        return remote(sum_send.at[peer(o)], sum_recv.at[seq], ss.at[o], sr.at[o], span, peer(o))

    own_sum = pltpu.make_async_copy(sum_send.at[seq], sum_recv.at[seq], ss.at[0])
    own_sum.start()
    for o in far_first:
        sum_copy(o).start()

    def qkv_copy(h, t, o):
        d = peer(o)
        if t == 1:
            src, dst = q_ref.at[:, :, head_cols(d, h)], qbuf.at[h, :, seq]
        else:
            src, dst = (k_ref, v_ref)[t // 2].at[:, head_cols(d, h)], (kbuf, vbuf)[t // 2].at[h, seq]
        i = h * 3 + t
        if o == 0:
            return pltpu.make_async_copy(src, dst, qkv_s.at[i, 0])
        return remote(src, dst, qkv_s.at[i, o], qkv_r.at[i, o], span, d)

    def qkv_arrival(h, t, o):
        s = source(o)
        dst = qbuf.at[h, :, s] if t == 1 else (kbuf, vbuf)[t // 2].at[h, s]
        return landed(dst, qkv_r.at[h * 3 + t, o])

    for h in range(hl):
        for t in range(3):
            for o in range(ns):
                qkv_copy(h, t, o).start()

    def qkv_wait(h):
        for t in range(3):
            qkv_copy(h, t, 0).wait()
            for o in range(1, ns):
                qkv_arrival(h, t, o).wait()

    to_row = lax.broadcasted_iota(jnp.int32, (2 * gr, 2 * gr), 0)
    from_row = lax.broadcasted_iota(jnp.int32, (2 * gr, 2 * gr), 1)
    is_value = (to_row >= gr).astype(jnp.int32)
    within = to_row - is_value * gr
    wanted = (within // groups) * (2 * groups) + is_value * groups + within % groups
    order = (from_row == wanted).astype(F32).astype(BF16)

    own_sum.wait()
    for o in reversed(far_first):
        landed(sum_recv.at[source(o)], sr.at[o]).wait()
    stacked = sum_recv[...].reshape(2 * gr, width)
    sorted_rows = jnp.dot(order, stacked, preferred_element_type=F32).astype(BF16)
    sk[0, x] = sorted_rows[:gr]
    sv[0, x] = sorted_rows[gr:]

    def k_down(k, i):
        return remote(sk.at[k - 1, i], sk.at[k, i], kds.at[k, i], kdr.at[k, i], zdn, seq)

    def k_up(k, i):
        return remote(sk.at[(nz + 1 - k) % nz, i], sk.at[nz - k, i], kus.at[k, i], kur.at[k, i], zup, seq)

    def v_down(k):
        return remote(sv.at[k - 1, x], sv.at[k, x], vds.at[k], vdr.at[k], zdn, seq)

    def v_up(k):
        return remote(sv.at[(nz + 1 - k) % nz, x], sv.at[nz - k, x], vus.at[k], vur.at[k], zup, seq)

    def v_side(slot, dx):
        return remote(sv.at[slot, x], sv.at[slot, x], vxs.at[slot, dx], vxr.at[slot, dx], x_span(dx), seq)

    def k_side(dx):
        return remote(sk.at[0, x], sk.at[0, x], kxs.at[dx], kxr.at[dx], x_span(dx), seq)

    def down_sends(k):
        return jnp.logical_and(z >= 1, z + k <= nz)

    def up_sends(k):
        return lax.rem(z - k + 1 + nz, nz) >= nz - nu

    def first_keys(i):
        @pl.when(down_sends(1))
        def _():
            k_down(1, i).start()

        @pl.when(up_sends(1))
        def _():
            k_up(1, i).start()

    for dx in sides:
        k_side(dx).start()

    @pl.when(down_sends(1))
    def _():
        v_down(1).start()

    @pl.when(up_sends(1))
    def _():
        v_up(1).start()

    first_keys(x)
    for dx in sides:
        v_side(0, dx).start()

    def blank(slot):
        sk[slot] = jnp.zeros(sk.shape[1:], BF16)
        sv[slot] = jnp.zeros(sv.shape[1:], BF16)

    for slot in range(1, nz):
        if slot <= nd:

            @pl.when(z + slot >= nz)
            def _():
                blank(slot)

        else:
            passes = up_sends(nz - slot + 1)

            @pl.when(jnp.logical_not(passes))
            def _():
                blank(slot)

            @pl.when(jnp.logical_and(passes, z + slot >= nz))
            def _():
                for dx in range(1, nx):
                    sv[slot, x_source(dx)] = jnp.zeros(sv.shape[2:], BF16)

    for dx in sides:
        landed(sk.at[0, x_source(dx)], kxr.at[dx]).wait()
        first_keys(x_source(dx))

    loads[2].wait()
    level = lev_ref[0]
    sigma = (level.astype(F32) + 1.0) / gin.shape[0]
    row_id = lax.broadcasted_iota(jnp.int32, gin.shape, 0)
    row = jnp.sum(jnp.where(row_id == level, gin[...].astype(F32), 0.0), axis=0, keepdims=True)
    coef[...] = jnp.broadcast_to(row * sigma, coef.shape)

    def relay_values(k):
        @pl.when(z + k <= nz - 1)
        def _():
            landed(sv.at[k, x], vdr.at[k]).wait()
            if k < nd:

                @pl.when(z >= 1)
                def _():
                    v_down(k + 1).start()

            for dx in range(1, nx):
                v_side(k, dx).start()

        if k <= nu:

            @pl.when(up_sends(k + 1))
            def _():
                landed(sv.at[nz - k, x], vur.at[k]).wait()
                if k < nu:
                    v_up(k + 1).start()

                @pl.when(k >= z + 1)
                def _():
                    for dx in range(1, nx):
                        v_side(nz - k, dx).start()

    def relay_keys(k, i):
        @pl.when(z + k <= nz - 1)
        def _():
            landed(sk.at[k, i], kdr.at[k, i]).wait()
            if k < nd:

                @pl.when(z >= 1)
                def _():
                    k_down(k + 1, i).start()

        if k <= nu:

            @pl.when(up_sends(k + 1))
            def _():
                landed(sk.at[nz - k, i], kur.at[k, i]).wait()
                if k < nu:
                    k_up(k + 1, i).start()

    def sides_ready(chunk):
        for slot in range(chunk * cs, (chunk + 1) * cs):

            @pl.when(z + slot <= nz - 1)
            def _():
                for dx in range(1, nx):
                    landed(sv.at[slot, x_source(dx)], vxr.at[slot, dx]).wait()

    def head_slice(h):
        return slice(h * HEAD_DIM, (h + 1) * HEAD_DIM)

    def score(h, j, k):
        q = qbuf[h, j].reshape(qn, HEAD_DIM)
        return lax.dot_general(q, k, (((1,), (1,)), ((), ())), preferred_element_type=F32)

    def own_step(h, j):
        s = score(h, j, kbuf[h].reshape(ns * tl, HEAD_DIM))
        top = jnp.max(s, axis=1, keepdims=True)
        p = jnp.exp2((s - top) * c_exp)
        l_buf[h, j] = jnp.broadcast_to(jnp.sum(p, axis=1, keepdims=True), (qn, HEAD_DIM))
        v = vbuf[h].reshape(ns * tl, HEAD_DIM)
        acc_buf[h, j] = jnp.dot(p.astype(BF16), v, preferred_element_type=F32)
        m_buf[h, j] = jnp.broadcast_to(top, (qn, HEAD_DIM))

    def past_step(h, j):
        count = nz * plane
        s = score(h, j, sk[:, :, :, head_slice(h)].reshape(count, HEAD_DIM))
        ahead = lax.broadcasted_iota(jnp.int32, (1, count), 1) // gr
        valid = jnp.logical_and(ahead > x, z * nx + ahead < nsp)
        s = s + jnp.where(valid, 0.0, -1e30)
        before = m_buf[h, j]
        top = jnp.maximum(before, jnp.max(s, axis=1, keepdims=True))
        p = jnp.exp2((s - top[:, :1]) * c_exp)
        factor = jnp.exp2((before - top) * c_exp)
        total = l_buf[h, j] * factor + jnp.sum(p, axis=1, keepdims=True)
        v = sv[:, :, :, head_slice(h)].reshape(count, HEAD_DIM)
        mixed = acc_buf[h, j] * factor + jnp.dot(p.astype(BF16), v, preferred_element_type=F32)
        o = (mixed / total).astype(BF16)
        obuf[j, h] = o.reshape(ns, rows, HEAD_DIM)

    def own_work(h):
        def run(pair):
            own_step(h, 2 * pair)
            own_step(h, 2 * pair + 1)

        return run

    def hop(k, work):
        relay_values(k)
        if work is None:
            for d in [0] + sides:
                relay_keys(k, x_source(d))
            return

        def step(pair, carry):
            for i in range(nx // 2):
                d = pair * (nx // 2) + i
                relay_keys(k, x_source(d))
            work(pair)
            return carry

        lax.fori_loop(0, CHUNKS // 2, step, 0)

    work_at = {2: 0, 5: 1} if nd == 8 else {}
    for k in range(1, nd + 1):
        if k in work_at:
            qkv_wait(work_at[k])
            hop(k, own_work(work_at[k]))
        else:
            hop(k, None)
    for h in range(hl):
        if h not in work_at.values():
            qkv_wait(h)
            own_work(h)(0)
            own_work(h)(1)
    for c in range(4):
        sides_ready(c)

    def out_copy(j, h, o):
        sems = os_.at[j, h, o], or_.at[j, h, o]
        return remote(obuf.at[j, h, peer(o)], att.at[j, h, seq], *sems, span, peer(o))

    def own_out(j, h):
        return pltpu.make_async_copy(obuf.at[j, h, seq], att.at[j, h, seq], os_.at[j, h, 0])

    def shift_copy(j):
        return remote(cbuf.at[j], out_ref.at[j], hs_.at[j], hr.at[j], nxt, seq)

    loads[3].wait()

    def second_pass(j):
        for h in range(hl):
            past_step(h, j)
            for o in far_first:
                out_copy(j, h, o).start()
            own_out(j, h).start()

    def finish(j):
        for h in range(hl):
            own_out(j, h).wait()
            for o in range(1, ns):
                landed(att.at[j, h, source(o)], or_.at[j, h, o]).wait()
        square = jnp.zeros((rows, HEAD_DIM), F32)
        for s in range(ns):
            for h in range(hl):
                a = att[j, h, s].astype(F32)
                square = square + a * a
        mean = jnp.sum(square, axis=1, keepdims=True) / (heads * HEAD_DIM)
        inverse = jnp.broadcast_to(lax.rsqrt(mean + 1e-06), (rows, HEAD_DIM))
        for s in range(ns):
            for h in range(hl):
                cols = slice((s * hl + h) * HEAD_DIM, (s * hl + h + 1) * HEAD_DIM)
                a = att[j, h, s].astype(F32)
                cleaned = lat[j, :, cols].astype(F32) - coef[:1, cols] * a * inverse
                cbuf[j, :, cols] = cleaned.astype(BF16)

        @pl.when(span < nsp - 1)
        def _():
            shift_copy(j).start()

    def tail(j, carry):
        @pl.when(j < CHUNKS)
        def _():
            second_pass(j)

        @pl.when(j >= 1)
        def _():
            finish(j - 1)

        return carry

    lax.fori_loop(0, CHUNKS + 1, tail, 0)

    @pl.when(span > 0)
    def _():
        for j in range(CHUNKS):
            landed(out_ref.at[j], hr.at[j]).wait()

    for h in range(hl):
        for t in range(3):
            for o in range(1, ns):
                qkv_copy(h, t, o).wait_send()
    for o in range(1, ns):
        sum_copy(o).wait_send()
    for dx in range(1, nx):
        k_side(dx).wait_send()
    for k in range(1, nd + 1):

        @pl.when(down_sends(k))
        def _():
            v_down(k).wait_send()
            for i in range(nx):
                k_down(k, i).wait_send()

    for k in range(1, nu + 1):

        @pl.when(up_sends(k))
        def _():
            v_up(k).wait_send()
            for i in range(nx):
                k_up(k, i).wait_send()

    for slot in range(nz):

        @pl.when(z + slot <= nz - 1)
        def _():
            for dx in range(1, nx):
                v_side(slot, dx).wait_send()

    for j in range(CHUNKS):
        for h in range(hl):
            for o in range(1, ns):
                out_copy(j, h, o).wait_send()

        @pl.when(span < nsp - 1)
        def _():
            shift_copy(j).wait_send()


def local(nz, nx, queries, keys, values, latent, fresh_noise, pool_weight, gate_table, levels):
    ns = lax.axis_size("seq")
    tl, channels = keys.shape
    heads = channels // HEAD_DIM
    hl = heads // ns
    width = hl * HEAD_DIM
    rows = tl // CHUNKS
    groups = tl // POOL
    gr = groups * ns
    qn = ns * rows
    nd = nz // 2
    split = (CHUNKS, rows, channels)
    vmem = pl.BlockSpec(memory_space=pltpu.VMEM)
    far = pl.BlockSpec(memory_space=pl.ANY)
    dma = pltpu.SemaphoreType.DMA
    out = pl.pallas_call(
        functools.partial(kernel, nz, nx, ns, heads),
        out_shape=jax.ShapeDtypeStruct(split, BF16),
        in_specs=[far, far, far, far, vmem, far, pl.BlockSpec(memory_space=pltpu.SMEM)],
        out_specs=far,
        scratch_shapes=[
            pltpu.VMEM((tl, channels), BF16),
            pltpu.VMEM((tl, channels), BF16),
            pltpu.VMEM(gate_table.shape, BF16),
            pltpu.VMEM((hl, CHUNKS, ns, rows, HEAD_DIM), BF16),
            pltpu.VMEM((hl, ns, tl, HEAD_DIM), BF16),
            pltpu.VMEM((hl, ns, tl, HEAD_DIM), BF16),
            pltpu.VMEM((ns, 2 * groups, width), BF16),
            pltpu.VMEM((ns, 2 * groups, width), BF16),
            pltpu.VMEM((nz, nx, gr, width), BF16),
            pltpu.VMEM((nz, nx, gr, width), BF16),
            pltpu.VMEM((hl, CHUNKS, qn, HEAD_DIM), F32),
            pltpu.VMEM((hl, CHUNKS, qn, HEAD_DIM), F32),
            pltpu.VMEM((hl, CHUNKS, qn, HEAD_DIM), F32),
            pltpu.VMEM((CHUNKS, hl, ns, rows, HEAD_DIM), BF16),
            pltpu.VMEM((CHUNKS, hl, ns, rows, HEAD_DIM), BF16),
            pltpu.VMEM(split, BF16),
            pltpu.VMEM(split, BF16),
            pltpu.VMEM((8, channels), F32),
            dma((3 * hl, ns)),
            dma((3 * hl, ns)),
            dma((4,)),
            dma((ns,)),
            dma((ns,)),
            dma((nx,)),
            dma((nx,)),
            dma((nd + 1, nx)),
            dma((nd + 1, nx)),
            dma((nd + 1, nx)),
            dma((nd + 1, nx)),
            dma((nd + 1,)),
            dma((nd + 1,)),
            dma((nd + 1,)),
            dma((nd + 1,)),
            dma((nz, nx)),
            dma((nz, nx)),
            dma((CHUNKS, hl, ns)),
            dma((CHUNKS, hl, ns)),
            dma((CHUNKS,)),
            dma((CHUNKS,)),
        ],
        compiler_params=pltpu.CompilerParams(
            collective_id=0, has_side_effects=True, vmem_limit_bytes=VMEM_LIMIT
        ),
        name="step",
    )(
        queries.reshape(split),
        keys,
        values,
        latent.reshape(split),
        pool_weight.T,
        gate_table,
        levels,
    )
    return jnp.where(lax.axis_index("span") == 0, fresh_noise, out.reshape(tl, channels))


def solution(mesh, nx=NX):
    placed = (
        P(("span", "seq"), None),
        P(("span", "seq"), None),
        P(("span", "seq"), None),
        P(("span", "seq"), None),
        P("seq", None),
        P(),
        P(),
        P("span"),
    )
    return jax.shard_map(
        functools.partial(local, mesh.shape["span"] // nx, nx),
        mesh=mesh,
        in_specs=placed,
        out_specs=P(("span", "seq"), None),
        check_vma=False,
    )
```

time: 105 us -> 86.8 us (0.83)
  Pallas kernels: 101 us -> 83.8 us
  local copies, waits for them, and re-layouts: 2.77 us -> 0.01 us
  other arithmetic: 0 us -> 2.1 us
    pallas_call x1, Pallas kernels: 101 us -> 83.8 us  [local(): pl.pallas_call(functools.partial(kernel, nz, nx, ns, heads), out_shape=ja...]
    unnamed x4 -> x2, local copies, waits for them, and re-layouts: 2.77 us -> 0.01 us
    select_n x0 -> x1, other arithmetic: none -> 2.1 us  [local(): jnp.where(lax.axis_index('span') == 0, fresh_noise, out.reshape(tl, chann...]
where the time goes in v2:
time: 86.8 us; the launch traced here: 86.6 us
  Pallas kernels  83.8 us (97%)
  other arithmetic  2.1 us (2%)
    pallas_call x1, Pallas kernels, local(): pl.pallas_call(functools.partial(kernel, nz, nx, ns, heads), out_shape=ja...  83.8 us
    select_n x1, other arithmetic, local(): jnp.where(lax.axis_index('span') == 0, fresh_noise, out.reshape(tl, chann...  2.1 us

profile of v2, /device:TPU:32, one launch (start us, length us, event | category | flops | bytes accessed | tf_op | source)
XLA Modules:
  0.0 86.6 jit_solution(16079788556951743057)
XLA Ops:
  0.7 0.0 copy-start
  0.7 83.8 %step.1 = bf16[4,32,3072]{2,1,0:T(8,128)(2,1)} custom-call(bf16[4,32,3072]{2,1,0:T(8,128)(2,1)} %bitcast.5, bf16[128,3072]{1,0:T(8,128)(2,1)} %k_ref.1, bf16[128,3072]{1,0:T(8,128)(2,1)} %v_ref.1, bf16[4,32,3072]{2,1,0:T(8,128)(2,1)} %bitcast.6, bf16[24,32]{1,0:T(8,128)(2,1)} %bitcast.7, bf16[64,3072]{1,0:T(8,128)(2,1)} %gate_ref.1, s32[1]{0:T(128)S(6)} %copy.9.lev_ref), custom_call_target="tpu_custom_call" | custom-call | tf_op jit(solution)/shard_map/step/pallas_call | solution.py:481
  84.4 0.0 copy-done
  84.5 2.1 %bitcast_select_fusion = bf16[128,3072]{1,0:T(8,128)(2,1)} fusion(bf16[128,3072]{1,0:T(8,128)(2,1)S(1)} %copy-done, bf16[4,32,3072]{2,1,0:T(8,128)(2,1)} %step.1, pred[]{:T(512)S(6)} %eq.3), kind=kLoop, calls=%fused_computation | loop fusion | flops 393216 | bytes 2359297 | tf_op jit(solution)/shard_map/jit(_where)/select_n | solution.py:540
Async XLA Ops:
  0.7 83.8 %copy-start = (bf16[128,3072]{1,0:T(8,128)(2,1)S(1)}, bf16[128,3072]{1,0:T(8,128)(2,1)}, u32[]{:S(2)}) copy-start(bf16[128,3072]{1,0:T(8,128)(2,1)} %param.12) | copy-start | bytes 2359300

commit v3 on v2

--- a/solution.py
+++ b/solution.py
@@ -75,9 +75,6 @@
         return pltpu.make_async_copy(src, dst, loc.at[i])
 
     loads = [load(0, k_ref, kin), load(1, v_ref, vin), load(2, gate_ref, gin), load(3, lat_ref, lat)]
-    for c in loads:
-        c.start()
-
     barrier = pltpu.get_barrier_semaphore()
 
     def greet(s, q):
@@ -89,6 +86,8 @@
         greet(s, seq)
     for dx in reversed(sides):
         greet(x_span(dx), seq)
+    for c in loads:
+        c.start()
 
     eye = lax.broadcasted_iota(jnp.int32, (POOL, POOL), 0) == lax.broadcasted_iota(jnp.int32, (POOL, POOL), 1)
     mixing = lax.dot_general(
@@ -240,7 +239,7 @@
     row = jnp.sum(jnp.where(row_id == level, gin[...].astype(F32), 0.0), axis=0, keepdims=True)
     coef[...] = jnp.broadcast_to(row * sigma, coef.shape)
 
-    def relay_values(k):
+    def relay_down(k):
         @pl.when(z + k <= nz - 1)
         def _():
             landed(sv.at[k, x], vdr.at[k]).wait()
@@ -252,34 +251,29 @@
 
             for dx in range(1, nx):
                 v_side(k, dx).start()
-
-        if k <= nu:
-
-            @pl.when(up_sends(k + 1))
+            for d in [0] + sides:
+                i = x_source(d)
+                landed(sk.at[k, i], kdr.at[k, i]).wait()
+                if k < nd:
+
+                    @pl.when(z >= 1)
+                    def _():
+                        k_down(k + 1, i).start()
+
+    def relay_up(k):
+        @pl.when(up_sends(k + 1))
+        def _():
+            landed(sv.at[nz - k, x], vur.at[k]).wait()
+            if k < nu:
+                v_up(k + 1).start()
+
+            @pl.when(k >= z + 1)
             def _():
-                landed(sv.at[nz - k, x], vur.at[k]).wait()
-                if k < nu:
-                    v_up(k + 1).start()
-
-                @pl.when(k >= z + 1)
-                def _():
-                    for dx in range(1, nx):
-                        v_side(nz - k, dx).start()
-
-    def relay_keys(k, i):
-        @pl.when(z + k <= nz - 1)
-        def _():
-            landed(sk.at[k, i], kdr.at[k, i]).wait()
-            if k < nd:
-
-                @pl.when(z >= 1)
-                def _():
-                    k_down(k + 1, i).start()
-
-        if k <= nu:
-
-            @pl.when(up_sends(k + 1))
-            def _():
+                for dx in range(1, nx):
+                    v_side(nz - k, dx).start()
+
+            for d in [0] + sides:
+                i = x_source(d)
                 landed(sk.at[nz - k, i], kur.at[k, i]).wait()
                 if k < nu:
                     k_up(k + 1, i).start()
@@ -331,31 +325,18 @@
 
         return run
 
-    def hop(k, work):
-        relay_values(k)
-        if work is None:
-            for d in [0] + sides:
-                relay_keys(k, x_source(d))
-            return
-
-        def step(pair, carry):
-            for i in range(nx // 2):
-                d = pair * (nx // 2) + i
-                relay_keys(k, x_source(d))
-            work(pair)
-            return carry
-
-        lax.fori_loop(0, CHUNKS // 2, step, 0)
-
-    work_at = {2: 0, 5: 1} if nd == 8 else {}
+    plan = {2: (0, 0), 3: (0, 1), 5: (1, 0), 6: (1, 1), 7: (2, 0), 8: (2, 1)} if nd == 8 else {}
     for k in range(1, nd + 1):
-        if k in work_at:
-            qkv_wait(work_at[k])
-            hop(k, own_work(work_at[k]))
-        else:
-            hop(k, None)
-    for h in range(hl):
-        if h not in work_at.values():
+        relay_down(k)
+        if k <= nu:
+            relay_up(k)
+        if k in plan:
+            h, pair = plan[k]
+            if pair == 0:
+                qkv_wait(h)
+            own_work(h)(pair)
+    if not plan:
+        for h in range(hl):
             qkv_wait(h)
             own_work(h)(0)
             own_work(h)(1)

time: 86.8 us -> 86.2 us (level)
  no operation moved by 1% of the time
where the time goes in v3:
time: 86.2 us; the launch traced here: 86 us
  Pallas kernels  83.2 us (97%)
  other arithmetic  2.1 us (2%)
    pallas_call x1, Pallas kernels, local(): pl.pallas_call(functools.partial(kernel, nz, nx, ns, heads), out_shape=ja...  83.2 us
    select_n x1, other arithmetic, local(): jnp.where(lax.axis_index('span') == 0, fresh_noise, out.reshape(tl, chann...  2.1 us

profile of v3, /device:TPU:32, one launch (start us, length us, event | category | flops | bytes accessed | tf_op | source)
XLA Modules:
  0.0 86.0 jit_solution(11584515021008833045)
XLA Ops:
  0.7 0.0 copy-start
  0.7 83.2 %step.1 = bf16[4,32,3072]{2,1,0:T(8,128)(2,1)} custom-call(bf16[4,32,3072]{2,1,0:T(8,128)(2,1)} %bitcast.5, bf16[128,3072]{1,0:T(8,128)(2,1)} %k_ref.1, bf16[128,3072]{1,0:T(8,128)(2,1)} %v_ref.1, bf16[4,32,3072]{2,1,0:T(8,128)(2,1)} %bitcast.6, bf16[24,32]{1,0:T(8,128)(2,1)} %bitcast.7, bf16[64,3072]{1,0:T(8,128)(2,1)} %gate_ref.1, s32[1]{0:T(128)S(6)} %copy.9.lev_ref), custom_call_target="tpu_custom_call" | custom-call | tf_op jit(solution)/shard_map/step/pallas_call | solution.py:462
  83.9 0.0 copy-done
  83.9 2.1 %bitcast_select_fusion = bf16[128,3072]{1,0:T(8,128)(2,1)} fusion(bf16[128,3072]{1,0:T(8,128)(2,1)S(1)} %copy-done, bf16[4,32,3072]{2,1,0:T(8,128)(2,1)} %step.1, pred[]{:T(512)S(6)} %eq.3), kind=kLoop, calls=%fused_computation | loop fusion | flops 393216 | bytes 2359297 | tf_op jit(solution)/shard_map/jit(_where)/select_n | solution.py:521
Async XLA Ops:
  0.7 83.2 %copy-start = (bf16[128,3072]{1,0:T(8,128)(2,1)S(1)}, bf16[128,3072]{1,0:T(8,128)(2,1)}, u32[]{:S(2)}) copy-start(bf16[128,3072]{1,0:T(8,128)(2,1)} %param.12) | copy-start | bytes 2359300
